TPU v7x, 512 devices: a whole 4x4x16 slice. The times are simulated.
512 devices in a mesh: ep: 64 (over z, y), os: 8 (over x, core).
Axes of the slice: x: 4, y: 4, z: 16, core: 2. Of those that a mesh axis runs over, the one named last changes fastest.
Arguments:
- tokens: bfloat16 [8192, 2048], P('ep', 'os'), may hold values from -6 to 6
- cotangent: bfloat16 [8192, 2048], P('ep', 'os'), may hold values from -6 to 6
- expert_ids: int32 [8192, 8], P('ep'), may hold values from 0 to 63, all different within a row; in each aligned block of 128 rows (0 to 127, 128 to 255, ...) at most 24 rows name the same one
- route_weight: float32 [8192, 8], P('ep'), may hold values from 0.1 to 1
- placement: int32 [64], replicated, may hold values from 0 to 63, each once
- swap_flags: int32 [2, 64], replicated, may hold values from 0 to 1, as said below
- params: bfloat16 [64, 3, 2048, 384], P('ep', None, 'os'), may hold values from -1 to 1
- first_moment: bfloat16 [64, 3, 2048, 384], P('ep', None, 'os'), may hold values from -6 to 6
- second_moment: bfloat16 [64, 3, 2048, 384], P('ep', None, 'os'), may hold values from 0.5 to 20
Outputs:
- mixed: bfloat16 [8192, 2048], P('ep', 'os')
- input_grad: bfloat16 [8192, 2048], P('ep', 'os')
- new_params: bfloat16 [64, 3, 2048, 384], P('ep', None, 'os')
- new_first: bfloat16 [64, 3, 2048, 384], P('ep', None, 'os')
- new_second: bfloat16 [64, 3, 2048, 384], P('ep', None, 'os')
Inputs may be any that keep to these rules, and one draw needn't show every extreme that they name: `expert_ids`: each row names 8 different experts; in each aligned block of 128 rows (the rows of one index of ep) no expert is named by more than 24 rows, a bound that some block reaches. `placement`: A permutation of the 64 expert ids. swap_flags[r, i] = swap_flags[r, i XOR 2^b_r] with b_0 = log2(64) - 1 and b_1 = 0.
All inputs are finite; a program needn't handle non-finite values.
Results may differ from a plain program's by a relative error of at most 0.023.
Values may be sent and summed in bfloat16 or wider, within the bound.
A program may use at most 64 MiB of HBM per device.

v0:
```python
import jax
import jax.numpy as jnp
from jax import lax
from jax.sharding import PartitionSpec as P

beta_first = 0.9
beta_second = 0.999
learn_rate = 0.01
adam_eps = 1e-08
adam_count = 10.0


def from_partner(value, axis, bit):
    return lax.ppermute(value, axis, [(i, i ^ 1 << bit) for i in range(lax.axis_size(axis))])


def adam_update(weight, first, second, grad):
    first_new = beta_first * first.astype(jnp.float32) + (1.0 - beta_first) * grad
    second_new = beta_second * second.astype(jnp.float32) + (1.0 - beta_second) * grad * grad
    first_hat = first_new / (1.0 - beta_first**adam_count)
    second_hat = second_new / (1.0 - beta_second**adam_count)
    weight_new = weight.astype(jnp.float32) - learn_rate * first_hat / (
        jnp.sqrt(second_hat) + adam_eps
    )
    return (
        weight_new.astype(jnp.bfloat16),
        first_new.astype(jnp.bfloat16),
        second_new.astype(jnp.bfloat16),
    )


def derivative(back, gate, up):
    sigma = jax.nn.sigmoid(gate)
    active = gate * sigma
    d_gate = (back * up * sigma * (1.0 + gate * (1.0 - sigma))).astype(jnp.bfloat16)
    d_up = (back * active).astype(jnp.bfloat16)
    return jnp.stack((d_gate, d_up), axis=1)


def activate(gate, up):
    sigma = jax.nn.sigmoid(gate)
    return (gate * sigma * up).astype(jnp.bfloat16)


def on_device(
    tokens,
    cotangent,
    expert_ids,
    route_weight,
    placement,
    swap_flags,
    params,
    first_moment,
    second_moment,
):
    experts = lax.axis_size("ep")
    mine = lax.axis_index("ep")
    tok_rows, shard = tokens.shape
    top = expert_ids.shape[1]
    capacity = max(2, 3 * tok_rows * top // (2 * experts))
    index = jnp.arange(experts, dtype=jnp.int32)
    bits = [experts.bit_length() - 2, 0]
    place = placement
    own_flags = []
    for rnd in range(len(bits)):
        partner = index ^ 1 << bits[rnd]
        chosen = swap_flags[rnd] == 1
        place = jnp.where(chosen, place[partner], place)
        own_flags.append(jnp.sum(jnp.where(index == mine, swap_flags[rnd], 0)) == 1)
    state = jnp.stack((params, first_moment, second_moment))
    for rnd in range(len(bits)):
        moved = from_partner(state, "ep", bits[rnd])
        state = jnp.where(own_flags[rnd], moved, state)
    weight = state[0, 0]
    flat_ids = expert_ids.reshape(-1)
    match = flat_ids[:, None] == place[None, :]
    dest = jnp.sum(jnp.where(match, index[None, :], 0), axis=1)
    counts = jnp.cumsum(match.astype(jnp.int32), axis=0)
    slot = jnp.sum(jnp.where(match, counts - 1, 0), axis=1)
    position = dest * capacity + slot
    num_rows = flat_ids.shape[0]
    table = (
        jnp.zeros((experts * capacity,), jnp.int32)
        .at[position]
        .set(jnp.arange(num_rows, dtype=jnp.int32) + 1)
    )
    filled = table > 0
    source = jnp.maximum(table - 1, 0)
    owner = source // top
    weights_flat = route_weight.reshape(-1)
    x_send = jnp.where(filled[:, None], tokens[owner], jnp.zeros((), jnp.bfloat16)).reshape(
        experts, capacity, shard
    )
    dy_send = jnp.where(
        filled[:, None], weights_flat[source][:, None] * cotangent[owner].astype(jnp.float32), 0.0
    )
    dy_send = dy_send.astype(jnp.bfloat16).reshape(experts, capacity, shard)
    x_recv = lax.all_to_all(x_send, "ep", split_axis=0, concat_axis=0, tiled=True)
    x_rows = x_recv.reshape(-1, shard)
    terms = jnp.einsum("rd,kdh->rkh", x_rows, weight[:2], preferred_element_type=jnp.float32)
    summed = lax.psum(terms.astype(jnp.bfloat16), "os").astype(jnp.float32)
    gate = summed[:, 0]
    up = summed[:, 1]
    hidden = activate(gate, up)
    rows_out = jnp.einsum(
        "rh,dh->rd", hidden, weight[2], preferred_element_type=jnp.float32
    ).astype(jnp.bfloat16)
    back_y = lax.all_to_all(
        rows_out.reshape(experts, capacity, shard), "ep", split_axis=0, concat_axis=0, tiled=True
    )
    dy_recv = lax.all_to_all(dy_send, "ep", split_axis=0, concat_axis=0, tiled=True)
    dy_rows = dy_recv.reshape(-1, shard)
    back_terms = jnp.einsum("rd,dh->rh", dy_rows, weight[2], preferred_element_type=jnp.float32)
    back = lax.psum(back_terms.astype(jnp.bfloat16), "os").astype(jnp.float32)
    deriv = derivative(back, gate, up)
    grad_in = jnp.einsum("rd,rkh->kdh", x_rows, deriv, preferred_element_type=jnp.float32)
    grad_out = jnp.einsum("rd,rh->dh", dy_rows, hidden, preferred_element_type=jnp.float32)
    grad = jnp.concatenate((grad_in, grad_out[None]), axis=0)
    rows_grad = jnp.einsum(
        "rkh,kdh->rd", deriv, weight[:2], preferred_element_type=jnp.float32
    ).astype(jnp.bfloat16)
    back_dx = lax.all_to_all(
        rows_grad.reshape(experts, capacity, shard), "ep", split_axis=0, concat_axis=0, tiled=True
    )
    picked_y = back_y.reshape(-1, shard)[position].reshape(tok_rows, top, shard)
    mixed = jnp.sum(route_weight[:, :, None] * picked_y.astype(jnp.float32), axis=1).astype(
        jnp.bfloat16
    )
    picked_dx = back_dx.reshape(-1, shard)[position].reshape(tok_rows, top, shard)
    input_grad = jnp.sum(picked_dx.astype(jnp.float32), axis=1).astype(jnp.bfloat16)
    first = state[1, 0]
    second = state[2, 0]
    new_params, new_first, new_second = adam_update(weight, first, second, grad)
    return (mixed, input_grad, new_params[None], new_first[None], new_second[None])


def solution(mesh):
    placed = (
        P("ep", "os"),
        P("ep", "os"),
        P("ep", None),
        P("ep", None),
        P(),
        P(),
        P("ep", None, "os", None),
        P("ep", None, "os", None),
        P("ep", None, "os", None),
    )
    return jax.shard_map(
        on_device,
        mesh=mesh,
        in_specs=placed,
        out_specs=(
            P("ep", "os"),
            P("ep", "os"),
            P("ep", None, "os", None),
            P("ep", None, "os", None),
            P("ep", None, "os", None),
        ),
        check_vma=False,
    )
```

profile of v0, /device:TPU:6, one launch (start us, length us, event | category | flops | bytes accessed | tf_op | source)
XLA Modules:
  0.0 528.3 jit_solution(16222571462099775276)
XLA Ops:
  12.7 18.0 %reduce-window.6 = s32[64,8,128]{2,1,0:T(8,128)S(1)} reduce-window(s32[64,8,128]{2,1,0:T(8,128)S(1)} %compare_convert_fusion, s32[]{:T(128)} %constant.22.clone.1), window={size=1x1x128 pad=0_0x0_0x127_0}, to_apply=%region_1.2 | reduce-window | flops 8323072 | bytes 524292 | tf_op jit(solution)/shard_map/reduce-window
  31.4 4.3 scatter_custom_fusion
  36.0 5.9 %gather_fusion.4 = f32[1536]{0:T(1024)S(1)} fusion(f32[1024]{0:T(1024)S(1)} %reshape.350, s32[2048]{0:T(1024)S(1)} %get-tuple-element.19), kind=kCustom, calls=%fused_computation.4 | custom fusion | bytes 18432 | tf_op jit(solution)/shard_map/gather | solution.py:95
  42.0 4.8 gather_fusion.5
  48.2 18.7 %all-to-all-start.2 = ((bf16[64,24,256]{2,1,0:T(8,128)(2,1)}), bf16[64,24,256]{2,1,0:T(8,128)(2,1)S(1)}, u32[]{:S(2)}, u32[]{:S(2)}) async-start(bf16[64,24,256]{2,1,0:T(8,128)(2,1)} %fusion.10), calls=%async_computation.2 | async-start | bytes 1572864 | tf_op jit(solution)/shard_map/all_to_all | solution.py:111
  66.9 1.4 pad_maximum_fusion.1
  68.4 12.3 %collective-permute-start = (bf16[3,1,3,256,384]{4,3,2,1,0:T(8,128)(2,1)}, bf16[3,1,3,256,384]{4,3,2,1,0:T(8,128)(2,1)}, u32[]{:S(2)}, u32[]{:S(2)}) collective-permute-start(bf16[3,1,3,256,384]{4,3,2,1,0:T(8,128)(2,1)} %pad_maximum_fusion.1), channel_id=1, source_target_pairs={{0,256},{8,264},{16,272},{24,280},{32,288},{40,296},{48,304},{56,3... | collective-permute-start | bytes 5308424 | tf_op jit(solution)/shard_map/ppermute | solution.py:14
  80.7 5.4 %gather_fusion.2 = bf16[1536,256]{1,0:T(8,128)(2,1)} fusion(bf16[128,256]{1,0:T(8,128)(2,1)S(1)} %copy-done.1, s32[2048]{0:T(1024)S(1)} %get-tuple-element.20), kind=kCustom, calls=%fused_computation.2 | custom fusion | bytes 1579008 | tf_op jit(solution)/shard_map/gather | solution.py:91
  86.0 2.3 broadcast_select_fusion.2
  88.4 21.0 %all-to-all-done.2 = bf16[64,24,256]{2,1,0:T(8,128)(2,1)S(1)} async-done(((bf16[64,24,256]{2,1,0:T(8,128)(2,1)}), bf16[64,24,256]{2,1,0:T(8,128)(2,1)S(1)}, u32[]{:S(2)}, u32[]{:S(2)}) %all-to-all-start.2) | async-done | bytes 786464 | tf_op jit(solution)/shard_map/all_to_all | solution.py:111
  109.4 127.0 %all-to-all-start = ((bf16[64,24,256]{2,1,0:T(8,128)(2,1)}), bf16[64,24,256]{2,1,0:T(8,128)(2,1)}, u32[]{:S(2)}, u32[]{:S(2)}) async-start(bf16[64,24,256]{2,1,0:T(8,128)(2,1)} %broadcast_select_fusion.2), calls=%async_computation | async-start | bytes 1572864 | tf_op jit(solution)/shard_map/all_to_all | solution.py:98
  237.1 3.0 broadcast_select_fusion
  240.1 3.6 collective-permute-start.1
  244.3 26.6 %collective-permute-done.1 = bf16[3,1,3,256,384]{4,3,2,1,0:T(8,128)(2,1)} collective-permute-done((bf16[3,1,3,256,384]{4,3,2,1,0:T(8,128)(2,1)}, bf16[3,1,3,256,384]{4,3,2,1,0:T(8,128)(2,1)}, u32[]{:S(2)}, u32[]{:S(2)}) %collective-permute-start.1) | collective-permute-done | bytes 1769504 | tf_op jit(solution)/shard_map/ppermute | solution.py:14
  271.0 2.7 broadcast_select_fusion.1
  273.6 1.7 convolution_convert_fusion.1
  275.3 21.1 %all-to-all-done = bf16[64,24,256]{2,1,0:T(8,128)(2,1)} async-done(((bf16[64,24,256]{2,1,0:T(8,128)(2,1)}), bf16[64,24,256]{2,1,0:T(8,128)(2,1)}, u32[]{:S(2)}, u32[]{:S(2)}) %all-to-all-start) | async-done | bytes 786464 | tf_op jit(solution)/shard_map/all_to_all | solution.py:98
  296.4 3.3 convolution_convert_fusion
  299.8 99.8 %all-reduce.3.cloned.1.call-done = (bf16[1536,2,384]{2,0,1:T(8,128)(2,1)}, bf16[1536,384]{1,0:T(8,128)(2,1)}) async-done(((bf16[1536,2,384]{2,0,1:T(8,128)(2,1)}, bf16[1536,384]{1,0:T(8,128)(2,1)}), (bf16[1536,2,384]{2,0,1:T(8,128)(2,1)}, bf16[1536,384]{1,0:T(8,128)(2,1)})) %all-reduce.3.cloned.1.call-update) | async-done | bytes 3538960 | tf_op jit(solution)/shard_map/psum | solution.py:101
  399.6 2.1 convert_element_type.133
  403.8 1.7 fusion
  405.5 15.6 %all-to-all-start.3 = ((bf16[64,24,256]{2,1,0:T(8,128)(2,1)}), bf16[64,24,256]{2,1,0:T(8,128)(2,1)S(1)}, u32[]{:S(2)}, u32[]{:S(2)}) async-start(bf16[64,24,256]{2,1,0:T(8,128)(2,1)} %bitcast.27), calls=%async_computation.3 | async-start | bytes 1572864 | tf_op jit(solution)/shard_map/all_to_all | solution.py:122
  421.2 3.0 multiply_convert_fusion
  424.2 2.4 convolution_convert_fusion.2
  426.6 38.7 %all-to-all-done.3 = bf16[64,24,256]{2,1,0:T(8,128)(2,1)S(1)} async-done(((bf16[64,24,256]{2,1,0:T(8,128)(2,1)}), bf16[64,24,256]{2,1,0:T(8,128)(2,1)S(1)}, u32[]{:S(2)}, u32[]{:S(2)}) %all-to-all-start.3) | async-done | bytes 786464 | tf_op jit(solution)/shard_map/all_to_all | solution.py:122
  465.3 6.5 %all-to-all-start.1 = ((bf16[64,24,256]{2,1,0:T(8,128)(2,1)}), bf16[64,24,256]{2,1,0:T(8,128)(2,1)S(1)}, u32[]{:S(2)}, u32[]{:S(2)}) async-start(bf16[64,24,256]{2,1,0:T(8,128)(2,1)} %bitcast.130), calls=%async_computation.1 | async-start | bytes 1572864 | tf_op jit(solution)/shard_map/all_to_all | solution.py:108
  471.8 1.9 convolution_bitcast_fusion.1
  473.8 2.2 fusion.12
  476.0 2.1 fusion.21
  478.0 3.9 gather_fusion.6
  483.0 33.5 %all-to-all-done.1 = bf16[64,24,256]{2,1,0:T(8,128)(2,1)S(1)} async-done(((bf16[64,24,256]{2,1,0:T(8,128)(2,1)}), bf16[64,24,256]{2,1,0:T(8,128)(2,1)S(1)}, u32[]{:S(2)}, u32[]{:S(2)}) %all-to-all-start.1) | async-done | bytes 786464 | tf_op jit(solution)/shard_map/all_to_all | solution.py:108
  516.5 3.9 gather_fusion.3
  (67 shorter events, 12.1 us)
Async XLA Ops:
  7.2 34.9 %copy-start = (bf16[128,256]{1,0:T(8,128)(2,1)S(1)}, bf16[128,256]{1,0:T(8,128)(2,1)}, u32[]{:S(2)}) copy-start(bf16[128,256]{1,0:T(8,128)(2,1)} %param.10) | copy-start | bytes 196612
  8.2 27.5 %copy-start.14 = (f32[128,8]{0,1:T(8,128)S(1)}, f32[128,8]{0,1:T(8,128)}, u32[]{:S(2)}) copy-start(f32[128,8]{0,1:T(8,128)} %param.12) | copy-start | bytes 12292
  46.8 20.1 %copy-start.6 = (bf16[1,3,256,384]{3,2,1,0:T(8,128)(2,1)S(1)}, bf16[1,3,256,384]{3,2,1,0:T(8,128)(2,1)}, u32[]{:S(2)}) copy-start(bf16[1,3,256,384]{3,2,1,0:T(8,128)(2,1)} %param.17) | copy-start | bytes 1769476
  46.8 20.1 %copy-start.7 = (bf16[1,3,256,384]{3,2,1,0:T(8,128)(2,1)S(1)}, bf16[1,3,256,384]{3,2,1,0:T(8,128)(2,1)}, u32[]{:S(2)}) copy-start(bf16[1,3,256,384]{3,2,1,0:T(8,128)(2,1)} %param.16) | copy-start | bytes 1769476
  46.8 20.1 %copy-start.8 = (bf16[1,3,256,384]{3,2,1,0:T(8,128)(2,1)S(1)}, bf16[1,3,256,384]{3,2,1,0:T(8,128)(2,1)}, u32[]{:S(2)}) copy-start(bf16[1,3,256,384]{3,2,1,0:T(8,128)(2,1)} %param.15) | copy-start | bytes 1769476
  48.2 61.2 %all-to-all-start.2 = ((bf16[64,24,256]{2,1,0:T(8,128)(2,1)}), bf16[64,24,256]{2,1,0:T(8,128)(2,1)S(1)}, u32[]{:S(2)}, u32[]{:S(2)}) async-start(bf16[64,24,256]{2,1,0:T(8,128)(2,1)} %fusion.10), calls=%async_computation.2 | async-start | bytes 1572864 | tf_op jit(solution)/shard_map/all_to_all | solution.py:111
  66.9 13.7 %copy-start.1 = (bf16[128,256]{1,0:T(8,128)(2,1)S(1)}, bf16[128,256]{1,0:T(8,128)(2,1)}, u32[]{:S(2)}) copy-start(bf16[128,256]{1,0:T(8,128)(2,1)} %param.9) | copy-start | bytes 196612
  68.4 168.7 %collective-permute-start = (bf16[3,1,3,256,384]{4,3,2,1,0:T(8,128)(2,1)}, bf16[3,1,3,256,384]{4,3,2,1,0:T(8,128)(2,1)}, u32[]{:S(2)}, u32[]{:S(2)}) collective-permute-start(bf16[3,1,3,256,384]{4,3,2,1,0:T(8,128)(2,1)} %pad_maximum_fusion.1), channel_id=1, source_target_pairs={{0,256},{8,264},{16,272},{24,280},{32,288},{40,296},{48,304},{56,3... | collective-permute-start | bytes 5308424 | tf_op jit(solution)/shard_map/ppermute | solution.py:14
  109.3 164.3 %copy-start.5 = (bf16[64,24,256]{2,1,0:T(8,128)(2,1)}, bf16[64,24,256]{2,1,0:T(8,128)(2,1)S(1)}, u32[]{:S(2)}) copy-start(bf16[64,24,256]{2,1,0:T(8,128)(2,1)S(1)} %all-to-all-done.2) | copy-start | bytes 2359300
  109.4 187.1 %all-to-all-start = ((bf16[64,24,256]{2,1,0:T(8,128)(2,1)}), bf16[64,24,256]{2,1,0:T(8,128)(2,1)}, u32[]{:S(2)}, u32[]{:S(2)}) async-start(bf16[64,24,256]{2,1,0:T(8,128)(2,1)} %broadcast_select_fusion.2), calls=%async_computation | async-start | bytes 1572864 | tf_op jit(solution)/shard_map/all_to_all | solution.py:98
  236.4 163.2 %all-reduce.3.cloned.1.call-start = ((), (), s32[]{:S(2)}) async-start(), calls=%async_computation.4 | async-start | bytes 7077888 | tf_op jit(solution)/shard_map/psum | solution.py:101
  240.1 30.9 %collective-permute-start.1 = (bf16[3,1,3,256,384]{4,3,2,1,0:T(8,128)(2,1)}, bf16[3,1,3,256,384]{4,3,2,1,0:T(8,128)(2,1)}, u32[]{:S(2)}, u32[]{:S(2)}) collective-permute-start(bf16[3,1,3,256,384]{4,3,2,1,0:T(8,128)(2,1)} %broadcast_select_fusion), channel_id=1, source_target_pairs={{0,8},{8,0},{16,24},{24,16},{32,40},{40,32},{48,56},{56,48},{64,72... | collective-permute-start | bytes 5308424 | tf_op jit(solution)/shard_map/ppermute | solution.py:14
  273.6 130.2 %copy-start.3 = (bf16[3,1,3,256,384]{4,3,2,1,0:T(8,128)(2,1)}, bf16[3,1,3,256,384]{4,3,2,1,0:T(8,128)(2,1)S(1)}, u32[]{:S(2)}) copy-start(bf16[3,1,3,256,384]{4,3,2,1,0:T(8,128)(2,1)S(1)} %broadcast_select_fusion.1) | copy-start | bytes 5308420
  399.6 2.1 copy-start.13
  401.6 2.1 copy-start.2
  403.8 1.7 copy-start.9
  403.8 1.7 copy-start.11
  405.5 59.8 %all-to-all-start.3 = ((bf16[64,24,256]{2,1,0:T(8,128)(2,1)}), bf16[64,24,256]{2,1,0:T(8,128)(2,1)S(1)}, u32[]{:S(2)}, u32[]{:S(2)}) async-start(bf16[64,24,256]{2,1,0:T(8,128)(2,1)} %bitcast.27), calls=%async_computation.3 | async-start | bytes 1572864 | tf_op jit(solution)/shard_map/all_to_all | solution.py:122
  465.3 51.2 %all-to-all-start.1 = ((bf16[64,24,256]{2,1,0:T(8,128)(2,1)}), bf16[64,24,256]{2,1,0:T(8,128)(2,1)S(1)}, u32[]{:S(2)}, u32[]{:S(2)}) async-start(bf16[64,24,256]{2,1,0:T(8,128)(2,1)} %bitcast.130), calls=%async_computation.1 | async-start | bytes 1572864 | tf_op jit(solution)/shard_map/all_to_all | solution.py:108
  471.8 1.9 copy-start.10
  471.8 1.9 copy-start.12
  473.7 2.2 copy-start.4
Sparse Core Ops, SparseCore 0:
  299.9 99.6 all-reduce.2
where the time goes:
time: 529 us; the launch traced here: 528 us
  waiting for transfers between devices  241 us (46%)
  starting transfers between devices  184 us (35%)
  other arithmetic  41.9 us (8%)
  local copies, waits for them, and re-layouts  32.8 us (6%)
  between operations  15.8 us (3%)
  matrix products  13.2 us (2%)
    all_to_all x1, starting transfers between devices, on_device(): lax.all_to_all(x_send, 'ep', split_axis=0, concat_axis=0, tiled=True)  127 us
    psum x1, waiting for transfers between devices, on_device(): summed = lax.psum(terms.astype(jnp.bfloat16), 'os').astype(jnp.float32)  99.8 us
    all_to_all x1, waiting for transfers between devices, on_device(): lax.all_to_all(rows_grad.reshape(experts, capacity, shard), 'ep', split_a...  38.7 us
    all_to_all x1, waiting for transfers between devices, on_device(): lax.all_to_all(rows_out.reshape(experts, capacity, shard), 'ep', split_ax...  33.5 us
    ppermute x2, waiting for transfers between devices, from_partner(): lax.ppermute(value, axis, [(i, i ^ 1 << bit) for i in range(lax.axis_size...  26.6 us
    all_to_all x1, waiting for transfers between devices, on_device(): lax.all_to_all(x_send, 'ep', split_axis=0, concat_axis=0, tiled=True)  21.1 us
    all_to_all x1, waiting for transfers between devices, on_device(): lax.all_to_all(dy_send, 'ep', split_axis=0, concat_axis=0, tiled=True)  21 us
    all_to_all x1, starting transfers between devices, on_device(): lax.all_to_all(dy_send, 'ep', split_axis=0, concat_axis=0, tiled=True)  18.7 us
  transfers between devices with their start and end apart: 7, of which 6 were waited for; matrix products, arithmetic and copies ran while one was open for 6% of the time, Pallas kernels for 0%

commit v1 on v0

--- a/solution.py
+++ b/solution.py
@@ -98,7 +98,7 @@
     x_recv = lax.all_to_all(x_send, "ep", split_axis=0, concat_axis=0, tiled=True)
     x_rows = x_recv.reshape(-1, shard)
     terms = jnp.einsum("rd,kdh->rkh", x_rows, weight[:2], preferred_element_type=jnp.float32)
-    summed = lax.psum(terms.astype(jnp.bfloat16), "os").astype(jnp.float32)
+    summed = jnp.sum(lax.all_gather(terms.astype(jnp.bfloat16), "os"), axis=0).astype(jnp.float32)
     gate = summed[:, 0]
     up = summed[:, 1]
     hidden = activate(gate, up)

time: 529 us -> 551 us (1.042)
  starting transfers between devices: 184 us -> 49.9 us
  blocking collectives: 0 us -> 79.2 us
  waiting for transfers between devices: 241 us -> 302 us
  other arithmetic: 41.9 us -> 57.6 us
    all_to_all x1, starting transfers between devices: 127 us -> 8.9 us  [on_device(): lax.all_to_all(x_send, 'ep', split_axis=0, concat_axis=0, tiled=True)]
    all_to_all x0 -> x1, blocking collectives: none -> 79.2 us  [on_device(): lax.all_to_all(dy_send, 'ep', split_axis=0, concat_axis=0, tiled=True)]
    all_to_all x1, waiting for transfers between devices: 21.1 us -> 74 us  [on_device(): lax.all_to_all(x_send, 'ep', split_axis=0, concat_axis=0, tiled=True)]
    psum x1, waiting for transfers between devices: 99.8 us -> 64.6 us  [on_device(): back = lax.psum(back_terms.astype(jnp.bfloat16), 'os').astype(jnp.float32)]
    ppermute x2, waiting for transfers between devices: 26.6 us -> 61.7 us  [from_partner(): lax.ppermute(value, axis, [(i, i ^ 1 << bit) for i in range(lax.axis_size...]
    all_gather x0 -> x1, waiting for transfers between devices: none -> 29.3 us  [on_device(): lax.all_gather(terms.astype(jnp.bfloat16), 'os')]
    all_to_all x1 -> x0, waiting for transfers between devices: 21 us -> none  [on_device(): lax.all_to_all(dy_send, 'ep', split_axis=0, concat_axis=0, tiled=True)]
    all_to_all x1 -> x0, starting transfers between devices: 18.7 us -> none  [on_device(): lax.all_to_all(dy_send, 'ep', split_axis=0, concat_axis=0, tiled=True)]
  transfers between devices with their start and end apart: 7 -> 7, of which waited for: 6 -> 7; matrix products, arithmetic and copies ran while one was open for 6% -> 15% of each run, Pallas kernels for 0% -> 0%
where the time goes in v1:
time: 551 us; the launch traced here: 550 us
  waiting for transfers between devices  302 us (55%)
  blocking collectives  79.2 us (14%)
  other arithmetic  57.6 us (10%)
  starting transfers between devices  49.9 us (9%)
  local copies, waits for them, and re-layouts  32.4 us (6%)
  between operations  15.8 us (3%)
  matrix products  13.1 us (2%)
    all_to_all x1, blocking collectives, on_device(): lax.all_to_all(dy_send, 'ep', split_axis=0, concat_axis=0, tiled=True)  79.2 us
    all_to_all x1, waiting for transfers between devices, on_device(): lax.all_to_all(x_send, 'ep', split_axis=0, concat_axis=0, tiled=True)  74 us
    psum x1, waiting for transfers between devices, on_device(): back = lax.psum(back_terms.astype(jnp.bfloat16), 'os').astype(jnp.float32)  64.6 us
    ppermute x2, waiting for transfers between devices, from_partner(): lax.ppermute(value, axis, [(i, i ^ 1 << bit) for i in range(lax.axis_size...  61.7 us
    all_to_all x1, waiting for transfers between devices, on_device(): lax.all_to_all(rows_grad.reshape(experts, capacity, shard), 'ep', split_a...  39.8 us
    all_to_all x1, waiting for transfers between devices, on_device(): lax.all_to_all(rows_out.reshape(experts, capacity, shard), 'ep', split_ax...  32.5 us
    all_gather x1, waiting for transfers between devices, on_device(): lax.all_gather(terms.astype(jnp.bfloat16), 'os')  29.3 us
    ppermute x2, starting transfers between devices, from_partner(): lax.ppermute(value, axis, [(i, i ^ 1 << bit) for i in range(lax.axis_size...  19.5 us
  transfers between devices with their start and end apart: 7, of which 7 were waited for; matrix products, arithmetic and copies ran while one was open for 15% of the time, Pallas kernels for 0%

profile of v1, /device:TPU:6, one launch (start us, length us, event | category | flops | bytes accessed | tf_op | source)
XLA Modules:
  0.0 550.1 jit_solution(15778246100385545811)
XLA Ops:
  7.2 2.9 pad_maximum_fusion.1
  10.2 15.7 %collective-permute-start = (bf16[3,1,3,256,384]{4,3,2,1,0:T(8,128)(2,1)}, bf16[3,1,3,256,384]{4,3,2,1,0:T(8,128)(2,1)S(1)}, u32[]{:S(2)}, u32[]{:S(2)}) collective-permute-start(bf16[3,1,3,256,384]{4,3,2,1,0:T(8,128)(2,1)} %pad_maximum_fusion.1), channel_id=1, source_target_pairs={{0,256},{8,264},{16,272},{24,280},{32,288},{40,296},{48,304},{56,3... | collective-permute-start | bytes 5308424 | tf_op jit(solution)/shard_map/ppermute | solution.py:14
  28.6 18.0 %reduce-window.6 = s32[64,8,128]{2,1,0:T(8,128)S(1)} reduce-window(s32[64,8,128]{2,1,0:T(8,128)S(1)} %compare_convert_fusion, s32[]{:T(128)} %constant.22.clone.1), window={size=1x1x128 pad=0_0x0_0x127_0}, to_apply=%region_1.2 | reduce-window | flops 8323072 | bytes 524292 | tf_op jit(solution)/shard_map/reduce-window
  47.3 4.3 scatter_custom_fusion
  51.8 5.4 gather_fusion.2
  57.2 2.4 broadcast_select_fusion.2
  59.6 8.9 %all-to-all-start = ((bf16[64,24,256]{2,1,0:T(8,128)(2,1)}), bf16[64,24,256]{2,1,0:T(8,128)(2,1)}, u32[]{:S(2)}, u32[]{:S(2)}) async-start(bf16[64,24,256]{2,1,0:T(8,128)(2,1)} %broadcast_select_fusion.2), calls=%async_computation | async-start | bytes 1572864 | tf_op jit(solution)/shard_map/all_to_all | solution.py:98
  69.2 32.6 %collective-permute-done = bf16[3,1,3,256,384]{4,3,2,1,0:T(8,128)(2,1)S(1)} collective-permute-done((bf16[3,1,3,256,384]{4,3,2,1,0:T(8,128)(2,1)}, bf16[3,1,3,256,384]{4,3,2,1,0:T(8,128)(2,1)S(1)}, u32[]{:S(2)}, u32[]{:S(2)}) %collective-permute-start) | collective-permute-done | bytes 1769504 | tf_op jit(solution)/shard_map/ppermute | solution.py:14
  101.8 3.0 broadcast_select_fusion
  104.8 3.8 collective-permute-start.1
  109.2 29.1 %collective-permute-done.1 = bf16[3,1,3,256,384]{4,3,2,1,0:T(8,128)(2,1)} collective-permute-done((bf16[3,1,3,256,384]{4,3,2,1,0:T(8,128)(2,1)}, bf16[3,1,3,256,384]{4,3,2,1,0:T(8,128)(2,1)}, u32[]{:S(2)}, u32[]{:S(2)}) %collective-permute-start.1) | collective-permute-done | bytes 1769504 | tf_op jit(solution)/shard_map/ppermute | solution.py:14
  138.3 2.6 broadcast_select_fusion.1
  140.8 74.0 %all-to-all-done = bf16[64,24,256]{2,1,0:T(8,128)(2,1)} async-done(((bf16[64,24,256]{2,1,0:T(8,128)(2,1)}), bf16[64,24,256]{2,1,0:T(8,128)(2,1)}, u32[]{:S(2)}, u32[]{:S(2)}) %all-to-all-start) | async-done | bytes 786464 | tf_op jit(solution)/shard_map/all_to_all | solution.py:98
  214.8 3.3 convolution_convert_fusion
  219.0 4.8 gather_fusion.5
  223.9 5.9 %gather_fusion.4 = f32[1536]{0:T(1024)S(1)} fusion(f32[1024]{0:T(1024)S(1)} %reshape.350, s32[2048]{0:T(1024)S(1)} %get-tuple-element.17), kind=kCustom, calls=%fused_computation.4 | custom fusion | bytes 18432 | tf_op jit(solution)/shard_map/gather | solution.py:95
  230.5 79.2 %all_to_all.20 = bf16[64,24,256]{2,1,0:T(8,128)(2,1)S(1)} all-to-all(bf16[64,24,256]{2,1,0:T(8,128)(2,1)S(1)} %fusion.10), channel_id=1, replica_groups=mesh['ep'=64,'os'=8] {'ep'}, dimensions={0} | all-to-all | bytes 1572864 | tf_op jit(solution)/shard_map/all_to_all | solution.py:111
  312.3 29.3 %all-gather.3.cloned.1.call-done = bf16[12288,2,384]{2,0,1:T(8,128)(2,1)} async-done(((bf16[1536,2,384]{2,0,1:T(8,128)(2,1)}), bf16[12288,2,384]{2,0,1:T(8,128)(2,1)}) %all-gather.3.cloned.1.call-update) | async-done | bytes 18874384 | tf_op jit(solution)/shard_map/all_gather | solution.py:101
  341.6 11.8 %reduce_sum.73 = bf16[1536,2,384]{2,0,1:T(8,128)(2,1)} reduce(bf16[8,1536,2,384]{3,1,0,2:T(8,128)(2,1)} %bitcast.120, bf16[]{:T(256)} %constant.64.clone.1), dimensions={0}, to_apply=%region_7.8 | reduce | flops 8257536 | bytes 21233666 | tf_op jit(solution)/shard_map/reduce_sum | solution.py:101
  353.4 4.1 convert_element_type.135
  357.5 64.6 %all-reduce.2.cloned.1.call-done = bf16[1536,384]{1,0:T(8,128)(2,1)} async-done(((bf16[1536,384]{1,0:T(8,128)(2,1)}), bf16[1536,384]{1,0:T(8,128)(2,1)}) %all-reduce.2.cloned.1.call-update) | async-done | bytes 1179664 | tf_op jit(solution)/shard_map/psum | solution.py:114
  422.1 3.9 fusion.18
  427.8 15.7 %all-to-all-start.3 = ((bf16[64,24,256]{2,1,0:T(8,128)(2,1)}), bf16[64,24,256]{2,1,0:T(8,128)(2,1)S(1)}, u32[]{:S(2)}, u32[]{:S(2)}) async-start(bf16[64,24,256]{2,1,0:T(8,128)(2,1)} %bitcast.28), calls=%async_computation.3 | async-start | bytes 1572864 | tf_op jit(solution)/shard_map/all_to_all | solution.py:122
  443.4 3.0 multiply_convert_fusion
  446.5 2.4 convolution_convert_fusion.2
  448.9 39.8 %all-to-all-done.3 = bf16[64,24,256]{2,1,0:T(8,128)(2,1)S(1)} async-done(((bf16[64,24,256]{2,1,0:T(8,128)(2,1)}), bf16[64,24,256]{2,1,0:T(8,128)(2,1)S(1)}, u32[]{:S(2)}, u32[]{:S(2)}) %all-to-all-start.3) | async-done | bytes 786464 | tf_op jit(solution)/shard_map/all_to_all | solution.py:122
  488.7 5.8 %all-to-all-start.1 = ((bf16[64,24,256]{2,1,0:T(8,128)(2,1)}), bf16[64,24,256]{2,1,0:T(8,128)(2,1)S(1)}, u32[]{:S(2)}, u32[]{:S(2)}) async-start(bf16[64,24,256]{2,1,0:T(8,128)(2,1)} %bitcast.132), calls=%async_computation.1 | async-start | bytes 1572864 | tf_op jit(solution)/shard_map/all_to_all | solution.py:108
  496.5 2.2 fusion.12
  498.7 2.1 fusion.21
  500.8 3.9 gather_fusion.6
  505.7 32.5 %all-to-all-done.1 = bf16[64,24,256]{2,1,0:T(8,128)(2,1)S(1)} async-done(((bf16[64,24,256]{2,1,0:T(8,128)(2,1)}), bf16[64,24,256]{2,1,0:T(8,128)(2,1)S(1)}, u32[]{:S(2)}, u32[]{:S(2)}) %all-to-all-start.1) | async-done | bytes 786464 | tf_op jit(solution)/shard_map/all_to_all | solution.py:108
  538.3 3.9 gather_fusion.3
  (72 shorter events, 13.4 us)
Async XLA Ops:
  7.2 44.6 %copy-start = (bf16[128,256]{1,0:T(8,128)(2,1)S(1)}, bf16[128,256]{1,0:T(8,128)(2,1)}, u32[]{:S(2)}) copy-start(bf16[128,256]{1,0:T(8,128)(2,1)} %param.9) | copy-start | bytes 196612
  7.2 18.7 %copy-start.13 = (s32[128,8]{0,1:T(8,128)S(1)}, s32[128,8]{0,1:T(8,128)}, u32[]{:S(2)}) copy-start(s32[128,8]{0,1:T(8,128)} %param.11) | copy-start | bytes 12292
  7.2 19.1 %copy-start.2 = (s32[64]{0:T(128)S(1)}, s32[64]{0:T(128)}, u32[]{:S(2)}) copy-start(s32[64]{0:T(128)} %param.13) | copy-start | bytes 772
  7.2 19.8 %copy-start.15 = (s32[2,64]{1,0:T(2,128)S(1)}, s32[2,64]{1,0:T(2,128)}, u32[]{:S(2)}) copy-start(s32[2,64]{1,0:T(2,128)} %param.14) | copy-start | bytes 1540
  10.2 91.6 %collective-permute-start = (bf16[3,1,3,256,384]{4,3,2,1,0:T(8,128)(2,1)}, bf16[3,1,3,256,384]{4,3,2,1,0:T(8,128)(2,1)S(1)}, u32[]{:S(2)}, u32[]{:S(2)}) collective-permute-start(bf16[3,1,3,256,384]{4,3,2,1,0:T(8,128)(2,1)} %pad_maximum_fusion.1), channel_id=1, source_target_pairs={{0,256},{8,264},{16,272},{24,280},{32,288},{40,296},{48,304},{56,3... | collective-permute-start | bytes 5308424 | tf_op jit(solution)/shard_map/ppermute | solution.py:14
  57.2 44.6 %copy-start.7 = (bf16[1,3,256,384]{3,2,1,0:T(8,128)(2,1)S(1)}, bf16[1,3,256,384]{3,2,1,0:T(8,128)(2,1)}, u32[]{:S(2)}) copy-start(bf16[1,3,256,384]{3,2,1,0:T(8,128)(2,1)} %param.17) | copy-start | bytes 1769476
  57.2 44.6 %copy-start.8 = (bf16[1,3,256,384]{3,2,1,0:T(8,128)(2,1)S(1)}, bf16[1,3,256,384]{3,2,1,0:T(8,128)(2,1)}, u32[]{:S(2)}) copy-start(bf16[1,3,256,384]{3,2,1,0:T(8,128)(2,1)} %param.16) | copy-start | bytes 1769476
  59.6 155.3 %all-to-all-start = ((bf16[64,24,256]{2,1,0:T(8,128)(2,1)}), bf16[64,24,256]{2,1,0:T(8,128)(2,1)}, u32[]{:S(2)}, u32[]{:S(2)}) async-start(bf16[64,24,256]{2,1,0:T(8,128)(2,1)} %broadcast_select_fusion.2), calls=%async_computation | async-start | bytes 1572864 | tf_op jit(solution)/shard_map/all_to_all | solution.py:98
  68.5 273.1 %all-gather.3.cloned.1.call-start = ((), (), s32[]{:S(2)}) async-start(), calls=%async_computation.5 | async-start | bytes 21233664 | tf_op jit(solution)/shard_map/all_gather | solution.py:101
  101.8 3.0 copy-start.6
  104.8 33.5 %collective-permute-start.1 = (bf16[3,1,3,256,384]{4,3,2,1,0:T(8,128)(2,1)}, bf16[3,1,3,256,384]{4,3,2,1,0:T(8,128)(2,1)}, u32[]{:S(2)}, u32[]{:S(2)}) collective-permute-start(bf16[3,1,3,256,384]{4,3,2,1,0:T(8,128)(2,1)} %broadcast_select_fusion), channel_id=1, source_target_pairs={{0,8},{8,0},{16,24},{24,16},{32,40},{40,32},{48,56},{56,48},{64,72... | collective-permute-start | bytes 5308424 | tf_op jit(solution)/shard_map/ppermute | solution.py:14
  140.8 285.2 %copy-start.3 = (bf16[3,1,3,256,384]{4,3,2,1,0:T(8,128)(2,1)}, bf16[3,1,3,256,384]{4,3,2,1,0:T(8,128)(2,1)S(1)}, u32[]{:S(2)}) copy-start(bf16[3,1,3,256,384]{4,3,2,1,0:T(8,128)(2,1)S(1)} %broadcast_select_fusion.1) | copy-start | bytes 5308420
  218.1 0.8 copy-start.1
  218.2 5.6 %copy-start.14 = (f32[128,8]{0,1:T(8,128)S(1)}, f32[128,8]{0,1:T(8,128)}, u32[]{:S(2)}) copy-start(f32[128,8]{0,1:T(8,128)} %param.12) | copy-start | bytes 12292
  218.2 203.9 %all-reduce.2.cloned.1.call-start = ((), (), s32[]{:S(2)}) async-start(), calls=%async_computation.4 | async-start | bytes 2359296 | tf_op jit(solution)/shard_map/psum | solution.py:114
  309.7 0.9 copy-start.5
  426.0 1.7 copy-start.9
  426.0 1.7 copy-start.11
  427.8 60.9 %all-to-all-start.3 = ((bf16[64,24,256]{2,1,0:T(8,128)(2,1)}), bf16[64,24,256]{2,1,0:T(8,128)(2,1)S(1)}, u32[]{:S(2)}, u32[]{:S(2)}) async-start(bf16[64,24,256]{2,1,0:T(8,128)(2,1)} %bitcast.28), calls=%async_computation.3 | async-start | bytes 1572864 | tf_op jit(solution)/shard_map/all_to_all | solution.py:122
  488.7 49.6 %all-to-all-start.1 = ((bf16[64,24,256]{2,1,0:T(8,128)(2,1)}), bf16[64,24,256]{2,1,0:T(8,128)(2,1)S(1)}, u32[]{:S(2)}, u32[]{:S(2)}) async-start(bf16[64,24,256]{2,1,0:T(8,128)(2,1)} %bitcast.132), calls=%async_computation.1 | async-start | bytes 1572864 | tf_op jit(solution)/shard_map/all_to_all | solution.py:108
  494.5 1.9 copy-start.10
  494.6 1.9 copy-start.12
  496.5 2.2 copy-start.4
Sparse Core Ops, SparseCore 0:
  218.3 123.2 all-gather.2
  343.9 78.1 all-reduce.1
